TPU v7x, 32 devices: a whole 2x2x4 slice. The times are simulated.
32 devices in a mesh: node: 16 (over z, y, core), chip: 2 (over x).
Axes of the slice: x: 2, y: 2, z: 4, core: 2. Of those that a mesh axis runs over, the one named last changes fastest.
Arguments:
- tokens: bfloat16 [256, 3584], P(('node', 'chip')), may hold values from -6 to 6
- expert_ids: int32 [256, 8], P(('node', 'chip')), may hold values from 0 to 31, as said below
- gate_values: bfloat16 [256, 8], P(('node', 'chip')), may hold values from 0.099609375 to 1
- slot_ids: int32 [256, 8], P(('node', 'chip')), may hold values from 0 to 7, as said below
- up_weight: bfloat16 [32, 3584, 1024], P('node', None, 'chip'), may hold values from -0.09375 to 0.09375
- down_weight: bfloat16 [32, 1024, 3584], P('node', 'chip'), may hold values from -0.1875 to 0.1875
Outputs:
- mixed: bfloat16 [256, 3584], P(('node', 'chip'))
Inputs may be any that keep to these rules, and one draw needn't show every extreme that they name: `expert_ids`: each token's 8 entries name, in some order, all 2 experts of each of 4 distinct nodes. `slot_ids`: entries of one token that name experts of the same node hold the same slot; among the 16 tokens of one node (aligned blocks of the token dimension), the slots to one destination node are distinct, and some destination node receives all 8 slots from each source node.
All inputs are finite; a program needn't handle non-finite values.
Results may differ from a plain program's by a relative error of at most 0.0058.
Values may be sent and summed in bfloat16 or wider, within the bound.
A program may use at most 64 MiB of HBM per device.

v0:
```python
import jax
import jax.numpy as jnp
from jax import lax
from jax.sharding import PartitionSpec as P


def pack_rows(targets, experts, node_tokens, node_gates, row_count, per_node):
    row_ids = jnp.arange(row_count, dtype=jnp.int32)
    matches = (targets[None, :, :] == row_ids[:, None, None]).astype(jnp.bfloat16)
    picked = jnp.minimum(jnp.sum(matches.astype(jnp.float32), axis=2), 1.0).astype(jnp.bfloat16)
    packed = jnp.dot(picked, node_tokens, preferred_element_type=jnp.float32).astype(jnp.bfloat16)
    choose = (experts[:, :, None] == jnp.arange(per_node, dtype=jnp.int32)[None, None, :]).astype(
        jnp.bfloat16
    )
    weighted = choose * node_gates[:, :, None]
    gate_rows = jnp.einsum(
        "rtk,tke->re", matches, weighted, preferred_element_type=jnp.float32
    ).astype(jnp.bfloat16)
    return (packed, gate_rows)


def expert_rows(row_block, gate_block, up_local, down_local):
    result = jnp.zeros((row_block.shape[0], down_local.shape[2]), jnp.float32)
    for expert in range(up_local.shape[0]):
        hidden = jax.nn.silu(
            jnp.dot(row_block, up_local[expert], preferred_element_type=jnp.float32)
        ).astype(jnp.bfloat16)
        product = jnp.dot(hidden, down_local[expert], preferred_element_type=jnp.float32)
        result = result + gate_block[:, expert : expert + 1].astype(jnp.float32) * product
    return result.astype(jnp.bfloat16)


def gather_sum(indices, table):
    valid = indices >= 0
    safe = jnp.where(valid, indices, 0).reshape(-1)
    picked = jnp.take(table, safe, axis=0).reshape(
        indices.shape[0], indices.shape[1], table.shape[1]
    )
    return jnp.sum(jnp.where(valid[:, :, None], picked, 0.0), axis=1)


def shards(tokens, expert_ids, gate_values, slot_ids, up_weight, down_weight):
    node_count = lax.axis_size("node")
    chip_count = lax.axis_size("chip")
    my_chip = lax.axis_index("chip")
    tok_dev = tokens.shape[0]
    model_dim = tokens.shape[1]
    per_node = up_weight.shape[0]
    capacity = 8 * chip_count * tok_dev // node_count
    block_cap = capacity // chip_count
    route_code = (expert_ids // per_node * capacity + slot_ids) * per_node + expert_ids % per_node
    node_tokens, node_gates = (
        lax.all_gather(tokens, "chip", axis=0, tiled=True),
        lax.all_gather(gate_values, "chip", axis=0, tiled=True),
    )
    node_codes = lax.all_gather(route_code, "chip", axis=0, tiled=True)
    node_expert = node_codes % per_node
    node_slot = node_codes // per_node % capacity
    node_dest = node_codes // per_node // capacity
    targets = node_dest * capacity + node_slot
    packed, gate_rows = pack_rows(
        targets, node_expert, node_tokens, node_gates, node_count * capacity, per_node
    )
    shaped = packed.reshape(node_count, chip_count, 1, block_cap, model_dim)
    gate_shaped = gate_rows.reshape(node_count, chip_count, 1, block_cap, per_node)
    arrived, arrived_gates = (
        lax.all_to_all(shaped, "node", split_axis=0, concat_axis=2, tiled=True),
        lax.all_to_all(gate_shaped, "node", split_axis=0, concat_axis=2, tiled=True),
    )
    row_block = arrived.reshape(-1, model_dim)
    gate_block = arrived_gates.reshape(-1, per_node)
    partial_value = expert_rows(row_block, gate_block, up_weight, down_weight)
    pieces = lax.all_to_all(
        partial_value.reshape(chip_count, node_count * block_cap, model_dim),
        "chip",
        split_axis=0,
        concat_axis=0,
        tiled=True,
    )
    slot_sums = jnp.sum(pieces.astype(jnp.float32), axis=0).reshape(
        node_count, block_cap, model_dim
    )
    held = lax.all_to_all(slot_sums, "node", split_axis=0, concat_axis=0, tiled=True).reshape(
        node_count * block_cap, model_dim
    )
    wanted = (node_slot // block_cap == my_chip) & (node_expert == 0)
    indices = jnp.where(wanted, node_dest * block_cap + node_slot % block_cap, -1)
    term = gather_sum(indices, held)
    summed = lax.psum_scatter(term, "chip", scatter_dimension=0, tiled=True)
    return summed.astype(jnp.bfloat16)


def solution(mesh):
    return jax.shard_map(
        shards,
        mesh=mesh,
        in_specs=(
            P(("node", "chip"), None),
            P(("node", "chip"), None),
            P(("node", "chip"), None),
            P(("node", "chip"), None),
            P("node", None, "chip"),
            P("node", "chip", None),
        ),
        out_specs=P(("node", "chip"), None),
        check_vma=False,
    )
```

profile of v0, /device:TPU:0, one launch (start us, length us, event | category | flops | bytes accessed | tf_op | source)
XLA Modules:
  0.0 136.6 jit_solution(9596992641009980675)
XLA Ops:
  6.5 0.7 fusion.38
  7.3 5.3 %all_gather.9 = s32[16,8]{1,0:T(8,128)S(1)} all-gather(s32[8,8]{1,0:T(8,128)S(1)} %fusion.38), channel_id=1, replica_groups=mesh['node'=16,'chip'=2] {'chip'}, dimensions={0}, use_global_device_ids=true | all-gather | bytes 768 | tf_op jit(solution)/shard_map/all_gather | solution.py:56
  12.5 4.6 %all_gather.10 = bf16[16,8]{1,0:T(8,128)(2,1)S(1)} all-gather(bf16[8,8]{1,0:T(8,128)(2,1)} %param.8), channel_id=1, replica_groups=mesh['node'=16,'chip'=2] {'chip'}, dimensions={0}, use_global_device_ids=true | all-gather | bytes 384 | tf_op jit(solution)/shard_map/all_gather | solution.py:54
  17.1 0.1 copy.18
  17.2 0.1 copy.17
  17.3 0.1 copy.16
  17.4 0.2 fusion.14
  17.6 0.1 reshape.70
  17.7 0.6 copy.19
  18.3 6.4 %all-to-all-start = ((bf16[16,2,1,4,2]{3,1,4,2,0:T(2,128)(2,1)}), bf16[16,2,1,4,2]{3,1,4,2,0:T(2,128)(2,1)S(1)}, u32[]{:S(2)}, u32[]{:S(2)}) async-start(bf16[16,2,1,4,2]{3,1,4,2,0:T(2,128)(2,1)} %copy.19), calls=%async_computation | async-start | bytes 32768 | tf_op jit(solution)/shard_map/all_to_all | solution.py:68
  24.7 0.1 convert_reduce_fusion.1
  24.8 5.1 %all_gather.11 = bf16[16,3584]{1,0:T(8,128)(2,1)S(1)} all-gather(bf16[8,3584]{1,0:T(8,128)(2,1)} %param.6), channel_id=1, replica_groups=mesh['node'=16,'chip'=2] {'chip'}, dimensions={0}, use_global_device_ids=true | all-gather | bytes 172032 | tf_op jit(solution)/shard_map/all_gather | solution.py:53
  29.9 0.4 convolution_convert_fusion
  30.4 1.1 reshape.72
  31.5 6.0 %all-to-all-start.1 = ((bf16[16,2,1,4,3584]{4,3,1,2,0:T(4,128)(2,1)}), bf16[16,2,1,4,3584]{4,3,1,2,0:T(4,128)(2,1)S(1)}, u32[]{:S(2)}, u32[]{:S(2)}) async-start(bf16[16,2,1,4,3584]{4,3,1,2,0:T(4,128)(2,1)} %bitcast.4), calls=%async_computation.1 | async-start | bytes 1835008 | tf_op jit(solution)/shard_map/all_to_all | solution.py:67
  37.5 0.1 reshape.71
  37.6 20.6 %all-to-all-done.1 = bf16[16,2,1,4,3584]{4,3,1,2,0:T(4,128)(2,1)S(1)} async-done(((bf16[16,2,1,4,3584]{4,3,1,2,0:T(4,128)(2,1)}), bf16[16,2,1,4,3584]{4,3,1,2,0:T(4,128)(2,1)S(1)}, u32[]{:S(2)}, u32[]{:S(2)}) %all-to-all-start.1) | async-done | bytes 917536 | tf_op jit(solution)/shard_map/all_to_all | solution.py:67
  58.3 0.3 copy.22
  58.6 0.2 reshape.73
  58.8 5.7 %convolution_multiply_fusion.1 = f32[128,3584]{1,0:T(8,128)} fusion(bf16[2,512,3584]{2,1,0:T(8,128)(2,1)} %param.11, f32[128]{0:T(128)S(1)} %get-tuple-element.10, bf16[128,3584]{1,0:T(8,128)(2,1)S(1)} %reshape.73, bf16[2,3584,512]{2,1,0:T(8,128)(2,1)} %param.10), kind=kOutput, calls=%fused_computation.3 | convolution fusion | flops 940310528 | bytes 10093056 | tf_op jit(solution)/shard_map/dot_general | solution.py:28
  64.5 4.9 %fusion.1 = bf16[128,3584]{1,0:T(8,128)(2,1)S(1)} fusion(f32[128,3584]{1,0:T(8,128)} %convolution_multiply_fusion.1, bf16[2,512,3584]{2,1,0:T(8,128)(2,1)} %param.11, f32[128]{0:T(128)S(1)} %get-tuple-element.9, bf16[128,3584]{1,0:T(8,128)(2,1)S(1)} %reshape.73, bf16[2,3584,512]{2,1,0:T(8,128)(2,1)} %param.10), kind=kOutput, calls=%fused_computation.4 | convolution fusion | flops 941228032 | bytes 11010560 | tf_op jit(solution)/shard_map/dot_general | solution.py:28
  69.5 15.6 %all_to_all.40 = bf16[2,64,3584]{2,1,0:T(8,128)(2,1)S(1)} all-to-all(bf16[2,64,3584]{2,1,0:T(8,128)(2,1)S(1)} %bitcast.58), channel_id=1, replica_groups=mesh['node'=16,'chip'=2] {'chip'}, dimensions={0} | all-to-all | bytes 1835008 | tf_op jit(solution)/shard_map/all_to_all | solution.py:73
  85.1 0.1 convert_reduce_fusion
  85.2 1.2 reshape.75
  86.4 5.9 %all-to-all-start.3 = ((f32[16,4,3584]{2,1,0:T(4,128)}), f32[16,4,3584]{2,1,0:T(4,128)S(1)}, u32[]{:S(2)}, u32[]{:S(2)}) async-start(f32[16,4,3584]{2,1,0:T(4,128)} %reshape.75), calls=%async_computation.3 | async-start | bytes 1835008 | tf_op jit(solution)/shard_map/all_to_all | solution.py:83
  92.5 0.1 reshape.77
  92.6 20.5 %all-to-all-done.3 = f32[16,4,3584]{2,1,0:T(4,128)S(1)} async-done(((f32[16,4,3584]{2,1,0:T(4,128)}), f32[16,4,3584]{2,1,0:T(4,128)S(1)}, u32[]{:S(2)}, u32[]{:S(2)}) %all-to-all-start.3) | async-done | bytes 917536 | tf_op jit(solution)/shard_map/all_to_all | solution.py:83
  113.1 0.3 reshape.76
  113.5 1.3 gather_fusion
  114.7 1.4 %fusion.13 = f32[16,3584]{1,0:T(8,128)} fusion(f32[128,3584]{1,0:T(8,128)S(1)} %gather_fusion, pred[16,8]{1,0:T(8,128)(4,1)S(1)} %compare_and_fusion, pred[16,8]{1,0:T(8,128)(4,1)S(1)} %get-tuple-element.5), kind=kLoop, calls=%fused_computation.18 | loop fusion | flops 1318912 | bytes 2064640 | tf_op jit(solution)/shard_map/reduce_sum | solution.py:39
  116.2 12.0 %reduce-scatter.2.cloned.1.call-done = f32[8,3584]{1,0:T(8,128)} async-done(((f32[16,3584]{1,0:T(8,128)}), f32[8,3584]{1,0:T(8,128)}) %reduce-scatter.2.cloned.1.call-update) | async-done | bytes 114704 | tf_op jit(solution)/shard_map/reduce_scatter | solution.py:89
  128.2 1.5 %convert_element_type.42 = bf16[8,3584]{1,0:T(8,128)(2,1)} convert(f32[8,3584]{1,0:T(8,128)} %reduce-scatter.2.cloned.1.call-done) | non-fusion elementwise | flops 28672 | bytes 172032 | tf_op jit(solution)/shard_map/convert_element_type | solution.py:90
  (11 shorter events, 0.2 us)
Async XLA Ops:
  18.3 13.2 %all-to-all-start = ((bf16[16,2,1,4,2]{3,1,4,2,0:T(2,128)(2,1)}), bf16[16,2,1,4,2]{3,1,4,2,0:T(2,128)(2,1)S(1)}, u32[]{:S(2)}, u32[]{:S(2)}) async-start(bf16[16,2,1,4,2]{3,1,4,2,0:T(2,128)(2,1)} %copy.19), calls=%async_computation | async-start | bytes 32768 | tf_op jit(solution)/shard_map/all_to_all | solution.py:68
  31.5 26.8 %all-to-all-start.1 = ((bf16[16,2,1,4,3584]{4,3,1,2,0:T(4,128)(2,1)}), bf16[16,2,1,4,3584]{4,3,1,2,0:T(4,128)(2,1)S(1)}, u32[]{:S(2)}, u32[]{:S(2)}) async-start(bf16[16,2,1,4,3584]{4,3,1,2,0:T(4,128)(2,1)} %bitcast.4), calls=%async_computation.1 | async-start | bytes 1835008 | tf_op jit(solution)/shard_map/all_to_all | solution.py:67
  86.4 26.7 %all-to-all-start.3 = ((f32[16,4,3584]{2,1,0:T(4,128)}), f32[16,4,3584]{2,1,0:T(4,128)S(1)}, u32[]{:S(2)}, u32[]{:S(2)}) async-start(f32[16,4,3584]{2,1,0:T(4,128)} %reshape.75), calls=%async_computation.3 | async-start | bytes 1835008 | tf_op jit(solution)/shard_map/all_to_all | solution.py:83
  92.4 35.9 %reduce-scatter.2.cloned.1.call-start = ((), (), s32[]{:S(2)}) async-start(), calls=%async_computation.5 | async-start | bytes 344064 | tf_op jit(solution)/shard_map/reduce_scatter | solution.py:89
Sparse Core Ops, SparseCore 0:
  116.3 11.8 reduce-scatter.1
where the time goes:
time: 137 us
  waiting for transfers between devices  53.3 us (39%)
  blocking collectives  30.6 us (22%)
  starting transfers between devices  18.4 us (13%)
  between operations  13.5 us (10%)
  matrix products  11.3 us (8%)
  local copies, waits for them, and re-layouts  5.6 us (4%)
  other arithmetic  3.99 us (3%)
    all_to_all x1, waiting for transfers between devices, shards(): lax.all_to_all(shaped, 'node', split_axis=0, concat_axis=2, tiled=True)  20.6 us
    all_to_all x1, waiting for transfers between devices, shards(): lax.all_to_all(slot_sums, 'node', split_axis=0, concat_axis=0, tiled=True)  20.5 us
    all_to_all x1, blocking collectives, shards(): lax.all_to_all(partial_value.reshape(chip_count, node_count * block_cap,...  15.6 us
    reduce_scatter x1, waiting for transfers between devices, shards(): summed = lax.psum_scatter(term, 'chip', scatter_dimension=0, tiled=True)  12 us
    dot_general x2, matrix products, expert_rows(): jnp.dot(hidden, down_local[expert], preferred_element_type=jnp.float32)  10.7 us
    all_to_all x1, starting transfers between devices, shards(): lax.all_to_all(gate_shaped, 'node', split_axis=0, concat_axis=2, tiled=True)  6.42 us
    all_to_all x1, starting transfers between devices, shards(): lax.all_to_all(shaped, 'node', split_axis=0, concat_axis=2, tiled=True)  5.97 us
    all_to_all x1, starting transfers between devices, shards(): lax.all_to_all(slot_sums, 'node', split_axis=0, concat_axis=0, tiled=True)  5.95 us
  transfers between devices with their start and end apart: 4, of which 3 were waited for; matrix products, arithmetic and copies ran while one was open for 1% of the time, Pallas kernels for 0%

commit v1 on v0

--- a/solution.py
+++ b/solution.py
@@ -2,6 +2,22 @@
 import jax.numpy as jnp
 from jax import lax
 from jax.sharding import PartitionSpec as P
+
+
+def pairwise_exchange(array, axis, split, join):
+    ways, here = (lax.axis_size(axis), lax.axis_index(axis))
+    width = array.shape[split] // ways
+    dims = list(array.shape)
+    dims[split] = width
+    height = dims[join]
+    dims[join] = height * ways
+    full = jnp.zeros(dims, array.dtype)
+    for mask in range(ways):
+        part = lax.dynamic_slice_in_dim(array, (here ^ mask) * width, width, axis=split)
+        if mask:
+            part = lax.ppermute(part, axis, [(d, d ^ mask) for d in range(ways)])
+        full = lax.dynamic_update_slice_in_dim(full, part, (here ^ mask) * height, axis=join)
+    return full
 
 
 def pack_rows(targets, experts, node_tokens, node_gates, row_count, per_node):
@@ -64,7 +80,7 @@
     shaped = packed.reshape(node_count, chip_count, 1, block_cap, model_dim)
     gate_shaped = gate_rows.reshape(node_count, chip_count, 1, block_cap, per_node)
     arrived, arrived_gates = (
-        lax.all_to_all(shaped, "node", split_axis=0, concat_axis=2, tiled=True),
+        pairwise_exchange(shaped, "node", 0, 2),
         lax.all_to_all(gate_shaped, "node", split_axis=0, concat_axis=2, tiled=True),
     )
     row_block = arrived.reshape(-1, model_dim)

time: 137 us -> 167 us (1.22)
  waiting for transfers between devices: 53.3 us -> 72.6 us
  starting transfers between devices: 18.4 us -> 28.9 us
    ppermute x0 -> x15, waiting for transfers between devices: none -> 40 us  [pairwise_exchange(): part = lax.ppermute(part, axis, [(d, d ^ mask) for d in range(ways)])]
    all_to_all x1 -> x0, waiting for transfers between devices: 20.6 us -> none  [shards(): lax.all_to_all(shaped, 'node', split_axis=0, concat_axis=2, tiled=True)]
    ppermute x0 -> x15, starting transfers between devices: none -> 18.8 us  [pairwise_exchange(): part = lax.ppermute(part, axis, [(d, d ^ mask) for d in range(ways)])]
    all_to_all x1 -> x0, starting transfers between devices: 5.97 us -> none  [shards(): lax.all_to_all(shaped, 'node', split_axis=0, concat_axis=2, tiled=True)]
    all_to_all x1, starting transfers between devices: 5.95 us -> 3.63 us  [shards(): lax.all_to_all(slot_sums, 'node', split_axis=0, concat_axis=0, tiled=True)]
  transfers between devices with their start and end apart: 4 -> 18, of which waited for: 3 -> 13; matrix products, arithmetic and copies ran while one was open for 1% -> 1% of each run, Pallas kernels for 0% -> 0%
where the time goes in v1:
time: 167 us; the launch traced here: 166 us
  waiting for transfers between devices  72.6 us (43%)
  blocking collectives  30.1 us (18%)
  starting transfers between devices  28.9 us (17%)
  between operations  13.7 us (8%)
  matrix products  11.3 us (7%)
  local copies, waits for them, and re-layouts  5.51 us (3%)
  other arithmetic  4.01 us (2%)
    ppermute x15, waiting for transfers between devices, pairwise_exchange(): part = lax.ppermute(part, axis, [(d, d ^ mask) for d in range(ways)])  40 us
    all_to_all x1, waiting for transfers between devices, shards(): lax.all_to_all(slot_sums, 'node', split_axis=0, concat_axis=0, tiled=True)  20.6 us
    ppermute x15, starting transfers between devices, pairwise_exchange(): part = lax.ppermute(part, axis, [(d, d ^ mask) for d in range(ways)])  18.8 us
    all_to_all x1, blocking collectives, shards(): lax.all_to_all(partial_value.reshape(chip_count, node_count * block_cap,...  15.2 us
    reduce_scatter x1, waiting for transfers between devices, shards(): summed = lax.psum_scatter(term, 'chip', scatter_dimension=0, tiled=True)  12 us
    dot_general x2, matrix products, expert_rows(): jnp.dot(hidden, down_local[expert], preferred_element_type=jnp.float32)  10.7 us
    all_to_all x1, starting transfers between devices, shards(): lax.all_to_all(gate_shaped, 'node', split_axis=0, concat_axis=2, tiled=True)  6.42 us
    all_gather x1, blocking collectives, shards(): node_codes = lax.all_gather(route_code, 'chip', axis=0, tiled=True)  5.28 us
  transfers between devices with their start and end apart: 18, of which 13 were waited for; matrix products, arithmetic and copies ran while one was open for 1% of the time, Pallas kernels for 0%

profile of v1, /device:TPU:0, one launch (start us, length us, event | category | flops | bytes accessed | tf_op | source)
XLA Modules:
  0.0 166.1 jit_solution(4830878216480357934)
XLA Ops:
  7.3 5.3 %all_gather.9 = s32[16,8]{1,0:T(8,128)S(1)} all-gather(s32[8,8]{1,0:T(8,128)S(1)} %fusion.38), channel_id=1, replica_groups=mesh['node'=16,'chip'=2] {'chip'}, dimensions={0}, use_global_device_ids=true | all-gather | bytes 768 | tf_op jit(solution)/shard_map/all_gather | solution.py:72
  12.5 4.6 %all_gather.10 = bf16[16,8]{1,0:T(8,128)(2,1)S(1)} all-gather(bf16[8,8]{1,0:T(8,128)(2,1)} %param.8), channel_id=1, replica_groups=mesh['node'=16,'chip'=2] {'chip'}, dimensions={0}, use_global_device_ids=true | all-gather | bytes 384 | tf_op jit(solution)/shard_map/all_gather | solution.py:70
  18.3 6.4 %all-to-all-start = ((bf16[16,2,1,4,2]{3,1,4,2,0:T(2,128)(2,1)}), bf16[16,2,1,4,2]{3,1,4,2,0:T(2,128)(2,1)S(1)}, u32[]{:S(2)}, u32[]{:S(2)}) async-start(bf16[16,2,1,4,2]{3,1,4,2,0:T(2,128)(2,1)} %copy.34), calls=%async_computation | async-start | bytes 32768 | tf_op jit(solution)/shard_map/all_to_all | solution.py:84
  24.9 5.1 %all_gather.11 = bf16[16,3584]{1,0:T(8,128)(2,1)S(1)} all-gather(bf16[8,3584]{1,0:T(8,128)(2,1)} %param.6), channel_id=1, replica_groups=mesh['node'=16,'chip'=2] {'chip'}, dimensions={0}, use_global_device_ids=true | all-gather | bytes 172032 | tf_op jit(solution)/shard_map/all_gather | solution.py:69
  31.4 3.2 %collective-permute-start.14 = (bf16[1,2,1,4,3584]{4,3,2,1,0:T(4,128)(2,1)S(1)}, bf16[1,2,1,4,3584]{4,3,2,1,0:T(4,128)(2,1)S(1)}, u32[]{:S(2)}, u32[]{:S(2)}) collective-permute-start(bf16[1,2,1,4,3584]{4,3,2,1,0:T(4,128)(2,1)S(1)} %get-tuple-element.7), channel_id=1, source_target_pairs={{0,30},{2,28},{4,26},{6,24},{8,22},{10,20},{12,18},{14,16},{16,14}... | collective-permute-start | bytes 172040 | tf_op jit(solution)/shard_map/ppermute | solution.py:18
  34.6 1.5 collective-permute-start.13
  36.1 3.2 %collective-permute-start.12 = (bf16[1,2,1,4,3584]{4,3,2,1,0:T(4,128)(2,1)S(1)}, bf16[1,2,1,4,3584]{4,3,2,1,0:T(4,128)(2,1)S(1)}, u32[]{:S(2)}, u32[]{:S(2)}) collective-permute-start(bf16[1,2,1,4,3584]{4,3,2,1,0:T(4,128)(2,1)S(1)} %get-tuple-element.9), channel_id=1, source_target_pairs={{0,26},{2,24},{4,30},{6,28},{8,18},{10,16},{12,22},{14,20},{16,10}... | collective-permute-start | bytes 172040 | tf_op jit(solution)/shard_map/ppermute | solution.py:18
  40.8 1.7 %collective-permute-start.1 = (bf16[1,2,1,4,3584]{4,3,2,1,0:T(4,128)(2,1)S(1)}, bf16[1,2,1,4,3584]{4,3,2,1,0:T(4,128)(2,1)S(1)}, u32[]{:S(2)}, u32[]{:S(2)}) collective-permute-start(bf16[1,2,1,4,3584]{4,3,2,1,0:T(4,128)(2,1)S(1)} %get-tuple-element.20), channel_id=1, source_target_pairs={{0,4},{2,6},{4,0},{6,2},{8,12},{10,14},{12,8},{14,10},{16,20},{18,... | collective-permute-start | bytes 172040 | tf_op jit(solution)/shard_map/ppermute | solution.py:18
  42.6 2.4 %collective-permute-done.1 = bf16[1,2,1,4,3584]{4,3,2,1,0:T(4,128)(2,1)S(1)} collective-permute-done((bf16[1,2,1,4,3584]{4,3,2,1,0:T(4,128)(2,1)S(1)}, bf16[1,2,1,4,3584]{4,3,2,1,0:T(4,128)(2,1)S(1)}, u32[]{:S(2)}, u32[]{:S(2)}) %collective-permute-start.1) | collective-permute-done | bytes 57376 | tf_op jit(solution)/shard_map/ppermute | solution.py:18
  45.6 3.3 %collective-permute-done.2 = bf16[1,2,1,4,3584]{4,3,2,1,0:T(4,128)(2,1)S(1)} collective-permute-done((bf16[1,2,1,4,3584]{4,3,2,1,0:T(4,128)(2,1)S(1)}, bf16[1,2,1,4,3584]{4,3,2,1,0:T(4,128)(2,1)S(1)}, u32[]{:S(2)}, u32[]{:S(2)}) %collective-permute-start.2) | collective-permute-done | bytes 57376 | tf_op jit(solution)/shard_map/ppermute | solution.py:18
  48.9 4.1 %collective-permute-done.3 = bf16[1,2,1,4,3584]{4,3,2,1,0:T(4,128)(2,1)S(1)} collective-permute-done((bf16[1,2,1,4,3584]{4,3,2,1,0:T(4,128)(2,1)S(1)}, bf16[1,2,1,4,3584]{4,3,2,1,0:T(4,128)(2,1)S(1)}, u32[]{:S(2)}, u32[]{:S(2)}) %collective-permute-start.3) | collective-permute-done | bytes 57376 | tf_op jit(solution)/shard_map/ppermute | solution.py:18
  53.1 3.6 %collective-permute-done.4 = bf16[1,2,1,4,3584]{4,3,2,1,0:T(4,128)(2,1)S(1)} collective-permute-done((bf16[1,2,1,4,3584]{4,3,2,1,0:T(4,128)(2,1)S(1)}, bf16[1,2,1,4,3584]{4,3,2,1,0:T(4,128)(2,1)S(1)}, u32[]{:S(2)}, u32[]{:S(2)}) %collective-permute-start.4) | collective-permute-done | bytes 57376 | tf_op jit(solution)/shard_map/ppermute | solution.py:18
  56.7 1.0 collective-permute-start.5
  57.7 4.1 %collective-permute-done.5 = bf16[1,2,1,4,3584]{4,3,2,1,0:T(4,128)(2,1)S(1)} collective-permute-done((bf16[1,2,1,4,3584]{4,3,2,1,0:T(4,128)(2,1)S(1)}, bf16[1,2,1,4,3584]{4,3,2,1,0:T(4,128)(2,1)S(1)}, u32[]{:S(2)}, u32[]{:S(2)}) %collective-permute-start.5) | collective-permute-done | bytes 57376 | tf_op jit(solution)/shard_map/ppermute | solution.py:18
  62.0 4.3 %collective-permute-done.6 = bf16[1,2,1,4,3584]{4,3,2,1,0:T(4,128)(2,1)S(1)} collective-permute-done((bf16[1,2,1,4,3584]{4,3,2,1,0:T(4,128)(2,1)S(1)}, bf16[1,2,1,4,3584]{4,3,2,1,0:T(4,128)(2,1)S(1)}, u32[]{:S(2)}, u32[]{:S(2)}) %collective-permute-start.6) | collective-permute-done | bytes 57376 | tf_op jit(solution)/shard_map/ppermute | solution.py:18
  66.3 2.9 %collective-permute-start.7 = (bf16[1,2,1,4,3584]{4,3,2,1,0:T(4,128)(2,1)S(1)}, bf16[1,2,1,4,3584]{4,3,2,1,0:T(4,128)(2,1)S(1)}, u32[]{:S(2)}, u32[]{:S(2)}) collective-permute-start(bf16[1,2,1,4,3584]{4,3,2,1,0:T(4,128)(2,1)S(1)} %get-tuple-element.14), channel_id=1, source_target_pairs={{0,16},{2,18},{4,20},{6,22},{8,24},{10,26},{12,28},{14,30},{16,0},... | collective-permute-start | bytes 172040 | tf_op jit(solution)/shard_map/ppermute | solution.py:18
  69.2 2.4 %collective-permute-done.7 = bf16[1,2,1,4,3584]{4,3,2,1,0:T(4,128)(2,1)S(1)} collective-permute-done((bf16[1,2,1,4,3584]{4,3,2,1,0:T(4,128)(2,1)S(1)}, bf16[1,2,1,4,3584]{4,3,2,1,0:T(4,128)(2,1)S(1)}, u32[]{:S(2)}, u32[]{:S(2)}) %collective-permute-start.7) | collective-permute-done | bytes 57376 | tf_op jit(solution)/shard_map/ppermute | solution.py:18
  71.6 1.1 collective-permute-start.8
  72.8 3.5 %collective-permute-done.8 = bf16[1,2,1,4,3584]{4,3,2,1,0:T(4,128)(2,1)S(1)} collective-permute-done((bf16[1,2,1,4,3584]{4,3,2,1,0:T(4,128)(2,1)S(1)}, bf16[1,2,1,4,3584]{4,3,2,1,0:T(4,128)(2,1)S(1)}, u32[]{:S(2)}, u32[]{:S(2)}) %collective-permute-start.8) | collective-permute-done | bytes 57376 | tf_op jit(solution)/shard_map/ppermute | solution.py:18
  76.3 2.8 %collective-permute-start.9 = (bf16[1,2,1,4,3584]{4,3,2,1,0:T(4,128)(2,1)S(1)}, bf16[1,2,1,4,3584]{4,3,2,1,0:T(4,128)(2,1)S(1)}, u32[]{:S(2)}, u32[]{:S(2)}) collective-permute-start(bf16[1,2,1,4,3584]{4,3,2,1,0:T(4,128)(2,1)S(1)} %get-tuple-element.12), channel_id=1, source_target_pairs={{0,20},{2,22},{4,16},{6,18},{8,28},{10,30},{12,24},{14,26},{16,4},... | collective-permute-start | bytes 172040 | tf_op jit(solution)/shard_map/ppermute | solution.py:18
  79.1 4.5 %collective-permute-done.9 = bf16[1,2,1,4,3584]{4,3,2,1,0:T(4,128)(2,1)S(1)} collective-permute-done((bf16[1,2,1,4,3584]{4,3,2,1,0:T(4,128)(2,1)S(1)}, bf16[1,2,1,4,3584]{4,3,2,1,0:T(4,128)(2,1)S(1)}, u32[]{:S(2)}, u32[]{:S(2)}) %collective-permute-start.9) | collective-permute-done | bytes 57376 | tf_op jit(solution)/shard_map/ppermute | solution.py:18
  83.6 7.0 %collective-permute-done.10 = bf16[1,2,1,4,3584]{4,3,2,1,0:T(4,128)(2,1)S(1)} collective-permute-done((bf16[1,2,1,4,3584]{4,3,2,1,0:T(4,128)(2,1)S(1)}, bf16[1,2,1,4,3584]{4,3,2,1,0:T(4,128)(2,1)S(1)}, u32[]{:S(2)}, u32[]{:S(2)}) %collective-permute-start.10) | collective-permute-done | bytes 57376 | tf_op jit(solution)/shard_map/ppermute | solution.py:18
  91.1 5.7 %convolution_multiply_fusion.1 = f32[128,3584]{1,0:T(8,128)} fusion(bf16[2,512,3584]{2,1,0:T(8,128)(2,1)} %param.11, f32[128]{0:T(128)S(1)} %get-tuple-element.26, bf16[128,3584]{1,0:T(8,128)(2,1)S(1)} %reshape.72, bf16[2,3584,512]{2,1,0:T(8,128)(2,1)} %param.10), kind=kOutput, calls=%fused_computation.3 | convolution fusion | flops 940310528 | bytes 10093056 | tf_op jit(solution)/shard_map/dot_general | solution.py:44
  96.8 4.9 %fusion.1 = bf16[128,3584]{1,0:T(8,128)(2,1)S(1)} fusion(f32[128,3584]{1,0:T(8,128)} %convolution_multiply_fusion.1, bf16[2,512,3584]{2,1,0:T(8,128)(2,1)} %param.11, f32[128]{0:T(128)S(1)} %get-tuple-element.25, bf16[128,3584]{1,0:T(8,128)(2,1)S(1)} %reshape.72, bf16[2,3584,512]{2,1,0:T(8,128)(2,1)} %param.10), kind=kOutput, calls=%fused_computation.4 | convolution fusion | flops 941228032 | bytes 11010560 | tf_op jit(solution)/shard_map/dot_general | solution.py:44
  101.8 15.2 %all_to_all.25 = bf16[2,64,3584]{2,1,0:T(8,128)(2,1)S(1)} all-to-all(bf16[2,64,3584]{2,1,0:T(8,128)(2,1)S(1)} %bitcast.68), channel_id=1, replica_groups=mesh['node'=16,'chip'=2] {'chip'}, dimensions={0} | all-to-all | bytes 1835008 | tf_op jit(solution)/shard_map/all_to_all | solution.py:89
  117.1 1.2 reshape.74
  118.3 3.6 %all-to-all-start.2 = ((f32[16,4,3584]{2,1,0:T(4,128)}), f32[16,4,3584]{2,1,0:T(4,128)S(1)}, u32[]{:S(2)}, u32[]{:S(2)}) async-start(f32[16,4,3584]{2,1,0:T(4,128)} %reshape.74), calls=%async_computation.2 | async-start | bytes 1835008 | tf_op jit(solution)/shard_map/all_to_all | solution.py:99
  122.1 20.6 %all-to-all-done.2 = f32[16,4,3584]{2,1,0:T(4,128)S(1)} async-done(((f32[16,4,3584]{2,1,0:T(4,128)}), f32[16,4,3584]{2,1,0:T(4,128)S(1)}, u32[]{:S(2)}, u32[]{:S(2)}) %all-to-all-start.2) | async-done | bytes 917536 | tf_op jit(solution)/shard_map/all_to_all | solution.py:99
  143.0 1.3 gather_fusion
  144.3 1.5 fusion.13
  145.8 12.0 %reduce-scatter.2.cloned.1.call-done = f32[8,3584]{1,0:T(8,128)} async-done(((f32[16,3584]{1,0:T(8,128)}), f32[8,3584]{1,0:T(8,128)}) %reduce-scatter.2.cloned.1.call-update) | async-done | bytes 114704 | tf_op jit(solution)/shard_map/reduce_scatter | solution.py:105
  157.8 1.5 convert_element_type.42
  (54 shorter events, 7.0 us)
Async XLA Ops:
  18.3 21.4 %all-to-all-start = ((bf16[16,2,1,4,2]{3,1,4,2,0:T(2,128)(2,1)}), bf16[16,2,1,4,2]{3,1,4,2,0:T(2,128)(2,1)S(1)}, u32[]{:S(2)}, u32[]{:S(2)}) async-start(bf16[16,2,1,4,2]{3,1,4,2,0:T(2,128)(2,1)} %copy.34), calls=%async_computation | async-start | bytes 32768 | tf_op jit(solution)/shard_map/all_to_all | solution.py:84
  31.4 59.4 %collective-permute-start.14 = (bf16[1,2,1,4,3584]{4,3,2,1,0:T(4,128)(2,1)S(1)}, bf16[1,2,1,4,3584]{4,3,2,1,0:T(4,128)(2,1)S(1)}, u32[]{:S(2)}, u32[]{:S(2)}) collective-permute-start(bf16[1,2,1,4,3584]{4,3,2,1,0:T(4,128)(2,1)S(1)} %get-tuple-element.7), channel_id=1, source_target_pairs={{0,30},{2,28},{4,26},{6,24},{8,22},{10,20},{12,18},{14,16},{16,14}... | collective-permute-start | bytes 172040 | tf_op jit(solution)/shard_map/ppermute | solution.py:18
  34.6 56.2 %collective-permute-start.13 = (bf16[1,2,1,4,3584]{4,3,2,1,0:T(4,128)(2,1)S(1)}, bf16[1,2,1,4,3584]{4,3,2,1,0:T(4,128)(2,1)S(1)}, u32[]{:S(2)}, u32[]{:S(2)}) collective-permute-start(bf16[1,2,1,4,3584]{4,3,2,1,0:T(4,128)(2,1)S(1)} %get-tuple-element.8), channel_id=1, source_target_pairs={{0,28},{2,30},{4,24},{6,26},{8,20},{10,22},{12,16},{14,18},{16,12}... | collective-permute-start | bytes 172040 | tf_op jit(solution)/shard_map/ppermute | solution.py:18
  36.1 54.6 %collective-permute-start.12 = (bf16[1,2,1,4,3584]{4,3,2,1,0:T(4,128)(2,1)S(1)}, bf16[1,2,1,4,3584]{4,3,2,1,0:T(4,128)(2,1)S(1)}, u32[]{:S(2)}, u32[]{:S(2)}) collective-permute-start(bf16[1,2,1,4,3584]{4,3,2,1,0:T(4,128)(2,1)S(1)} %get-tuple-element.9), channel_id=1, source_target_pairs={{0,26},{2,24},{4,30},{6,28},{8,18},{10,16},{12,22},{14,20},{16,10}... | collective-permute-start | bytes 172040 | tf_op jit(solution)/shard_map/ppermute | solution.py:18
  39.3 51.4 %collective-permute-start.11 = (bf16[1,2,1,4,3584]{4,3,2,1,0:T(4,128)(2,1)S(1)}, bf16[1,2,1,4,3584]{4,3,2,1,0:T(4,128)(2,1)S(1)}, u32[]{:S(2)}, u32[]{:S(2)}) collective-permute-start(bf16[1,2,1,4,3584]{4,3,2,1,0:T(4,128)(2,1)S(1)} %get-tuple-element.10), channel_id=1, source_target_pairs={{0,24},{2,26},{4,28},{6,30},{8,16},{10,18},{12,20},{14,22},{16,8},... | collective-permute-start | bytes 172040 | tf_op jit(solution)/shard_map/ppermute | solution.py:18
  39.5 1.2 collective-permute-start
  40.8 4.2 %collective-permute-start.1 = (bf16[1,2,1,4,3584]{4,3,2,1,0:T(4,128)(2,1)S(1)}, bf16[1,2,1,4,3584]{4,3,2,1,0:T(4,128)(2,1)S(1)}, u32[]{:S(2)}, u32[]{:S(2)}) collective-permute-start(bf16[1,2,1,4,3584]{4,3,2,1,0:T(4,128)(2,1)S(1)} %get-tuple-element.20), channel_id=1, source_target_pairs={{0,4},{2,6},{4,0},{6,2},{8,12},{10,14},{12,8},{14,10},{16,20},{18,... | collective-permute-start | bytes 172040 | tf_op jit(solution)/shard_map/ppermute | solution.py:18
  45.0 3.9 %collective-permute-start.2 = (bf16[1,2,1,4,3584]{4,3,2,1,0:T(4,128)(2,1)S(1)}, bf16[1,2,1,4,3584]{4,3,2,1,0:T(4,128)(2,1)S(1)}, u32[]{:S(2)}, u32[]{:S(2)}) collective-permute-start(bf16[1,2,1,4,3584]{4,3,2,1,0:T(4,128)(2,1)S(1)} %get-tuple-element.19), channel_id=1, source_target_pairs={{0,6},{2,4},{4,2},{6,0},{8,14},{10,12},{12,10},{14,8},{16,22},{18,... | collective-permute-start | bytes 172040 | tf_op jit(solution)/shard_map/ppermute | solution.py:18
  48.9 4.2 %collective-permute-start.3 = (bf16[1,2,1,4,3584]{4,3,2,1,0:T(4,128)(2,1)S(1)}, bf16[1,2,1,4,3584]{4,3,2,1,0:T(4,128)(2,1)S(1)}, u32[]{:S(2)}, u32[]{:S(2)}) collective-permute-start(bf16[1,2,1,4,3584]{4,3,2,1,0:T(4,128)(2,1)S(1)} %get-tuple-element.18), channel_id=1, source_target_pairs={{0,8},{2,10},{4,12},{6,14},{8,0},{10,2},{12,4},{14,6},{16,24},{18,... | collective-permute-start | bytes 172040 | tf_op jit(solution)/shard_map/ppermute | solution.py:18
  53.1 3.6 %collective-permute-start.4 = (bf16[1,2,1,4,3584]{4,3,2,1,0:T(4,128)(2,1)S(1)}, bf16[1,2,1,4,3584]{4,3,2,1,0:T(4,128)(2,1)S(1)}, u32[]{:S(2)}, u32[]{:S(2)}) collective-permute-start(bf16[1,2,1,4,3584]{4,3,2,1,0:T(4,128)(2,1)S(1)} %get-tuple-element.17), channel_id=1, source_target_pairs={{0,10},{2,8},{4,14},{6,12},{8,2},{10,0},{12,6},{14,4},{16,26},{18,... | collective-permute-start | bytes 172040 | tf_op jit(solution)/shard_map/ppermute | solution.py:18
  56.7 5.1 %collective-permute-start.5 = (bf16[1,2,1,4,3584]{4,3,2,1,0:T(4,128)(2,1)S(1)}, bf16[1,2,1,4,3584]{4,3,2,1,0:T(4,128)(2,1)S(1)}, u32[]{:S(2)}, u32[]{:S(2)}) collective-permute-start(bf16[1,2,1,4,3584]{4,3,2,1,0:T(4,128)(2,1)S(1)} %get-tuple-element.16), channel_id=1, source_target_pairs={{0,12},{2,14},{4,8},{6,10},{8,4},{10,6},{12,0},{14,2},{16,28},{18,... | collective-permute-start | bytes 172040 | tf_op jit(solution)/shard_map/ppermute | solution.py:18
  61.8 4.5 %collective-permute-start.6 = (bf16[1,2,1,4,3584]{4,3,2,1,0:T(4,128)(2,1)S(1)}, bf16[1,2,1,4,3584]{4,3,2,1,0:T(4,128)(2,1)S(1)}, u32[]{:S(2)}, u32[]{:S(2)}) collective-permute-start(bf16[1,2,1,4,3584]{4,3,2,1,0:T(4,128)(2,1)S(1)} %get-tuple-element.15), channel_id=1, source_target_pairs={{0,14},{2,12},{4,10},{6,8},{8,6},{10,4},{12,2},{14,0},{16,30},{18,... | collective-permute-start | bytes 172040 | tf_op jit(solution)/shard_map/ppermute | solution.py:18
  66.3 5.3 %collective-permute-start.7 = (bf16[1,2,1,4,3584]{4,3,2,1,0:T(4,128)(2,1)S(1)}, bf16[1,2,1,4,3584]{4,3,2,1,0:T(4,128)(2,1)S(1)}, u32[]{:S(2)}, u32[]{:S(2)}) collective-permute-start(bf16[1,2,1,4,3584]{4,3,2,1,0:T(4,128)(2,1)S(1)} %get-tuple-element.14), channel_id=1, source_target_pairs={{0,16},{2,18},{4,20},{6,22},{8,24},{10,26},{12,28},{14,30},{16,0},... | collective-permute-start | bytes 172040 | tf_op jit(solution)/shard_map/ppermute | solution.py:18
  71.6 4.7 %collective-permute-start.8 = (bf16[1,2,1,4,3584]{4,3,2,1,0:T(4,128)(2,1)S(1)}, bf16[1,2,1,4,3584]{4,3,2,1,0:T(4,128)(2,1)S(1)}, u32[]{:S(2)}, u32[]{:S(2)}) collective-permute-start(bf16[1,2,1,4,3584]{4,3,2,1,0:T(4,128)(2,1)S(1)} %get-tuple-element.13), channel_id=1, source_target_pairs={{0,18},{2,16},{4,22},{6,20},{8,26},{10,24},{12,30},{14,28},{16,2},... | collective-permute-start | bytes 172040 | tf_op jit(solution)/shard_map/ppermute | solution.py:18
  76.3 7.3 %collective-permute-start.9 = (bf16[1,2,1,4,3584]{4,3,2,1,0:T(4,128)(2,1)S(1)}, bf16[1,2,1,4,3584]{4,3,2,1,0:T(4,128)(2,1)S(1)}, u32[]{:S(2)}, u32[]{:S(2)}) collective-permute-start(bf16[1,2,1,4,3584]{4,3,2,1,0:T(4,128)(2,1)S(1)} %get-tuple-element.12), channel_id=1, source_target_pairs={{0,20},{2,22},{4,16},{6,18},{8,28},{10,30},{12,24},{14,26},{16,4},... | collective-permute-start | bytes 172040 | tf_op jit(solution)/shard_map/ppermute | solution.py:18
  83.6 7.1 %collective-permute-start.10 = (bf16[1,2,1,4,3584]{4,3,2,1,0:T(4,128)(2,1)S(1)}, bf16[1,2,1,4,3584]{4,3,2,1,0:T(4,128)(2,1)S(1)}, u32[]{:S(2)}, u32[]{:S(2)}) collective-permute-start(bf16[1,2,1,4,3584]{4,3,2,1,0:T(4,128)(2,1)S(1)} %get-tuple-element.11), channel_id=1, source_target_pairs={{0,22},{2,20},{4,18},{6,16},{8,30},{10,28},{12,26},{14,24},{16,6},... | collective-permute-start | bytes 172040 | tf_op jit(solution)/shard_map/ppermute | solution.py:18
  118.3 24.4 %all-to-all-start.2 = ((f32[16,4,3584]{2,1,0:T(4,128)}), f32[16,4,3584]{2,1,0:T(4,128)S(1)}, u32[]{:S(2)}, u32[]{:S(2)}) async-start(f32[16,4,3584]{2,1,0:T(4,128)} %reshape.74), calls=%async_computation.2 | async-start | bytes 1835008 | tf_op jit(solution)/shard_map/all_to_all | solution.py:99
  121.9 35.8 %reduce-scatter.2.cloned.1.call-start = ((), (), s32[]{:S(2)}) async-start(), calls=%async_computation.4 | async-start | bytes 344064 | tf_op jit(solution)/shard_map/reduce_scatter | solution.py:105
Sparse Core Ops, SparseCore 0:
  145.9 11.8 reduce-scatter.1
